TPU v7x, 32 devices: a whole 2x2x4 slice. The times are simulated.
32 devices in a mesh: req: 2 (over x), ctx: 4 (over y, core), tp: 4 (over z).
Axes of the slice: x: 2, y: 2, z: 4, core: 2. Of those that a mesh axis runs over, the one named last changes fastest.
Arguments:
- queries: bfloat16 [512, 16, 128], P('req', 'tp'), may hold values from -5 to 5
- new_keys: bfloat16 [512, 4, 128], P('req', 'tp'), may hold values from -5 to 5
- new_values: bfloat16 [512, 4, 128], P('req', 'tp'), may hold values from -24 to 24
- cache_keys: bfloat16 [2, 8192, 4, 128], P('req', 'ctx', 'tp'), may hold values from -5 to 5
- cache_values: bfloat16 [2, 8192, 4, 128], P('req', 'ctx', 'tp'), may hold values from -24 to 24
- cache_lengths: int32 [2], replicated, may hold values from 1 to 8192, as said below
- residual: bfloat16 [512, 2048], P(('req', 'ctx'), 'tp'), may hold values from -24 to 24
- out_weight: bfloat16 [2048, 2048], P('tp', 'ctx'), may hold values from -0.52734375 to 0.52734375
- norm_gain: float32 [2048], replicated, may hold values from 0.1 to 1.9
- expert_ids: int32 [512, 6], P(('req', 'ctx')), may hold values from 0 to 63, all different within a row; in each aligned block of 64 rows (0 to 63, 64 to 127, ...) at most 8 rows name the same one
- gate_weights: float32 [512, 6], P(('req', 'ctx')), may hold values from 0.1 to 1
- w_gate: bfloat16 [64, 2048, 1408], P('req', 'ctx', 'tp'), may hold values from -0.125 to 0.125
- w_up: bfloat16 [64, 2048, 1408], P('req', 'ctx', 'tp'), may hold values from -0.125 to 0.125
- w_down: bfloat16 [64, 1408, 2048], P('req', 'tp', 'ctx'), may hold values from -0.15625 to 0.15625
Outputs:
- layer_out: bfloat16 [512, 2048], P(('req', 'ctx'), 'tp')
Inputs may be any that keep to these rules, and one draw needn't show every extreme that they name: `cache_lengths`: the longest cached length equals 8192. `expert_ids`: within each aligned block of 64 tokens no expert is named by more than 8 routes, a bound that some block reaches.
All inputs are finite; a program needn't handle non-finite values.
Results may differ from a plain program's by a relative error of at most 0.006.
Values may be sent and summed in bfloat16 or wider, within the bound.
A program may use at most 384 MiB of HBM per device.

v0:
```python
import jax
import jax.numpy as jnp
from jax import lax
from jax.sharding import PartitionSpec as P

HD = 128
TOP = 6
CAP = 8
masked_score = -1e30


def merged_2(value, axis, join):
    pieces = jax.tree.map(lambda part: lax.all_gather(part, axis), value)
    head = jax.tree.map(lambda part: part[0], pieces)
    tail = jax.tree.map(lambda part: part[1:], pieces)
    so_far, _ = lax.scan(lambda so_far, piece: (join(so_far, piece), None), head, tail)
    return so_far


def joined_outputs(left_part, right_portion):
    highest = jnp.maximum(left_part[0], right_portion[0])
    left_factor = jnp.exp(left_part[0] - highest)
    right_factor = jnp.exp(right_portion[0] - highest)
    totals = left_part[1] * left_factor + right_portion[1] * right_factor
    numerator = left_part[2] * left_factor[..., None] + right_portion[2] * right_factor[..., None]
    return (highest, totals, numerator)


def body(
    queries,
    new_keys,
    new_values,
    cache_keys,
    cache_values,
    cache_lengths,
    residual,
    out_weight,
    norm_gain,
    expert_ids,
    gate_weights,
    w_gate,
    w_up,
    w_down,
):
    ctx_pos = lax.axis_index("ctx")
    tp_pos = lax.axis_index("tp")
    req_pos = lax.axis_index("req")
    ctx_count = lax.axis_size("ctx")
    tp_count = lax.axis_size("tp")
    req_count = lax.axis_size("req")
    tok_dev, head_count, head_size = queries.shape
    cache_dev = cache_keys.shape[1]
    model_width = w_down.shape[2] * ctx_count
    d_share = residual.shape[1]
    expert_mixture_device = tok_dev // ctx_count
    scale = 1.0 / HD**0.5
    query_flat = queries.reshape(tok_dev * head_count, head_size)
    key_rows = jnp.concatenate([cache_keys[0, :, 0, :], new_keys[:, 0, :]], 0)
    value_rows = jnp.concatenate([cache_values[0, :, 0, :], new_values[:, 0, :]], 0)
    length = lax.dynamic_index_in_dim(cache_lengths, req_pos, 0, keepdims=False)
    cache_valid = ctx_pos * cache_dev + jnp.arange(cache_dev, dtype=jnp.int32) < length
    is_last = ctx_pos == ctx_count - 1
    positions = jnp.arange(tok_dev, dtype=jnp.int32)
    causal = jnp.logical_and(positions[None, :] <= positions[:, None], is_last)
    valid = jnp.concatenate(
        [jnp.broadcast_to(cache_valid[None, :], (tok_dev, cache_dev)), causal], 1
    )
    scores = jnp.dot(query_flat, key_rows.T, preferred_element_type=jnp.float32) * scale
    scores = scores.reshape(tok_dev, head_count, cache_dev + tok_dev)
    scores = jnp.where(valid[:, None, :], scores, masked_score)
    local_max = jnp.max(scores, -1)
    probabilities = jnp.where(valid[:, None, :], jnp.exp(scores - local_max[..., None]), 0.0)
    local_sum = jnp.sum(probabilities, -1)
    rounded = probabilities.astype(jnp.bfloat16)
    numerator = jnp.einsum("thk,kd->thd", rounded, value_rows, preferred_element_type=jnp.float32)
    row_start = ctx_pos * expert_mixture_device
    col_start = tp_pos * d_share
    highest, totals, merged = merged_2((local_max, local_sum, numerator), "ctx", joined_outputs)
    attention_result = merged / totals[..., None]
    attention_result = lax.dynamic_slice_in_dim(
        attention_result, row_start, expert_mixture_device, 0
    )
    attention_result = attention_result.astype(jnp.bfloat16).reshape(
        expert_mixture_device, head_count * head_size
    )
    partial_value = jnp.dot(
        attention_result,
        lax.all_gather(out_weight, "ctx", axis=1, tiled=True),
        preferred_element_type=jnp.float32,
    )
    corner = lax.dynamic_slice_in_dim(partial_value, col_start, d_share, 1) + residual.astype(
        jnp.float32
    )
    partial_value = lax.dynamic_update_slice(partial_value, corner, (jnp.int32(0), col_start))
    hidden = lax.psum(partial_value, "tp")
    mean_square = jnp.mean(hidden * hidden, -1, keepdims=True)
    normed = (hidden * lax.rsqrt(mean_square + 1e-06) * norm_gain).astype(jnp.bfloat16)
    full_gate, full_up, full_down = (
        lax.all_gather(w_gate, "ctx", axis=1, tiled=True),
        lax.all_gather(w_up, "ctx", axis=1, tiled=True),
        lax.all_gather(w_down, "ctx", axis=2, tiled=True),
    )
    exp_dev = w_gate.shape[0]
    experts_all = exp_dev * req_count
    flat_ids = expert_ids.reshape(-1)
    route_count = flat_ids.shape[0]
    matches = (flat_ids[:, None] == jnp.arange(experts_all, dtype=jnp.int32)[None, :]).astype(
        jnp.int32
    )
    rank_in = jnp.sum(jnp.cumsum(matches, 0) * matches, 1) - 1
    slot_index = flat_ids * CAP + rank_in
    source = jnp.arange(route_count, dtype=jnp.int32) // TOP
    outgoing = (
        jnp.zeros((experts_all * CAP, model_width), jnp.bfloat16).at[slot_index].set(normed[source])
    )
    outgoing = outgoing.reshape(req_count, exp_dev, CAP, model_width)
    gathered = lax.all_to_all(outgoing, "req", split_axis=0, concat_axis=0, tiled=True)
    gate_act = jnp.einsum("resd,edf->resf", gathered, full_gate, preferred_element_type=jnp.float32)
    up_act = jnp.einsum("resd,edf->resf", gathered, full_up, preferred_element_type=jnp.float32)
    inner = (jax.nn.silu(gate_act) * up_act).astype(jnp.bfloat16)
    down_act = jnp.einsum("resf,efd->resd", inner, full_down, preferred_element_type=jnp.float32)
    expert_out = down_act.astype(jnp.bfloat16)
    returned_rows = lax.all_to_all(
        lax.all_to_all(expert_out, "req", split_axis=0, concat_axis=0, tiled=True),
        "tp",
        split_axis=3,
        concat_axis=2,
        tiled=True,
    )
    slot_sums = (
        returned_rows.reshape(req_count, exp_dev, tp_count, CAP, d_share).astype(jnp.float32).sum(2)
    )
    slot_sums = slot_sums.reshape(experts_all * CAP, d_share)
    picked = slot_sums[slot_index] * gate_weights.reshape(-1)[:, None]
    expert_mixture = picked.reshape(expert_mixture_device, TOP, d_share).sum(1)
    residual_part = lax.dynamic_slice_in_dim(hidden, col_start, d_share, 1)
    return (residual_part + expert_mixture).astype(jnp.bfloat16)


def solution(mesh):
    in_specs = (
        P("req", "tp", None),
        P("req", "tp", None),
        P("req", "tp", None),
        P("req", "ctx", "tp", None),
        P("req", "ctx", "tp", None),
        P(),
        P(("req", "ctx"), "tp"),
        P("tp", "ctx"),
        P(),
        P(("req", "ctx"), None),
        P(("req", "ctx"), None),
        P("req", "ctx", "tp"),
        P("req", "ctx", "tp"),
        P("req", "tp", "ctx"),
    )
    out_specs = P(("req", "ctx"), "tp")
    return jax.shard_map(body, mesh=mesh, in_specs=in_specs, out_specs=out_specs, check_vma=False)
```

profile of v0, /device:TPU:0, one launch (start us, length us, event | category | flops | bytes accessed | tf_op | source)
XLA Modules:
  0.0 1105.6 jit_solution(16539856928096114020)
XLA Ops:
  6.6 1.3 dynamic_slice.24
  7.9 0.7 add_compare_fusion
  8.7 3.5 broadcast_in_dim.48.clone
  12.2 5.6 broadcast_in_dim.49
  17.8 6.7 fusion.14
  24.7 11.4 %reshape.151 = f32[256,4,2304]{2,1,0:T(4,128)} reshape(f32[1024,2304]{1,0:T(8,128)} %get-tuple-element.92) | data formatting | bytes 18874368 | tf_op jit(solution)/shard_map/reshape | solution.py:69
  36.1 8.0 fusion.15
  44.2 0.7 all-gather.7.cloned.1.call-update
  45.1 5.3 select_reduce_fusion
  50.6 6.2 all_gather.33
  56.9 5.9 all_gather.31
  62.8 6.9 all-gather.15.cloned.1.call-done
  69.7 1.1 slice.40
  70.8 0.3 copy.69
  71.1 1.1 slice-done
  72.2 4.9 while.14
  72.5 1.3 fusion.75
  74.2 1.3 fusion.75
  75.9 1.3 fusion.75
  77.5 16.4 %all-gather.7.cloned.1.call-done = bf16[512,2048]{1,0:T(8,128)(2,1)} async-done(((bf16[512,512]{1,0:T(8,128)(2,1)}), bf16[512,2048]{1,0:T(8,128)(2,1)}) %all-gather.7.cloned.1.call-update) | async-done | bytes 2097168 | tf_op jit(solution)/shard_map/all_gather | solution.py:88
  93.9 2.1 fusion.59
  96.0 0.8 copy-done.2
  96.9 0.5 all-gather.9.cloned.1.call-update
  97.5 0.5 all-gather.11.cloned.1.call-update
  98.1 0.5 all-gather.13.cloned.1.call-update
  99.1 0.9 reduce-window.6
  100.7 34.6 %all-reduce.2.cloned.1.call-done = f32[64,2048]{1,0:T(8,128)} async-done(((f32[64,2048]{1,0:T(8,128)}), f32[64,2048]{1,0:T(8,128)}) %all-reduce.2.cloned.1.call-update) | async-done | bytes 524304 | tf_op jit(solution)/shard_map/psum | solution.py:95
  135.3 1.2 multiply_reduce_fusion.1
  136.5 1.2 multiply_convert_fusion
  137.7 9.7 scatter_custom_fusion
  147.3 28.3 %all_to_all.19 = bf16[2,32,8,2048]{3,2,1,0:T(8,128)(2,1)S(1)} all-to-all(bf16[2,32,8,2048]{3,2,1,0:T(8,128)(2,1)} %bitcast.108), channel_id=1, replica_groups=mesh['req'=2,'ctx'=4,'tp'=4] {'req'}, dimensions={0} | all-to-all | bytes 4194304 | tf_op jit(solution)/shard_map/all_to_all | solution.py:117
  175.6 234.8 %all-gather.9.cloned.1.call-done = bf16[32,2048,352]{1,2,0:T(8,128)(2,1)} async-done(((bf16[32,512,352]{1,2,0:T(8,128)(2,1)}), bf16[32,2048,352]{1,2,0:T(8,128)(2,1)}) %all-gather.9.cloned.1.call-update) | async-done | bytes 46137360 | tf_op jit(solution)/shard_map/all_gather | solution.py:99
  410.4 24.8 %fusion.28 = f32[2,32,8,352]{3,2,0,1:T(8,128)S(1)} fusion(bf16[32,2048,352]{1,2,0:T(8,128)(2,1)} %all-gather.9.cloned.1.call-done, bf16[2,32,8,2048]{3,2,1,0:T(8,128)(2,1)S(1)} %all_to_all.19), kind=kOutput, calls=%fused_computation.38 | convolution fusion | flops 738197504 | bytes 48955392 | tf_op jit(solution)/shard_map/resd,edf->resf/dot_general | solution.py:118
  435.1 250.3 %all-gather.11.cloned.1.call-done = bf16[32,2048,352]{1,2,0:T(8,128)(2,1)} async-done(((bf16[32,512,352]{1,2,0:T(8,128)(2,1)}), bf16[32,2048,352]{1,2,0:T(8,128)(2,1)}) %all-gather.11.cloned.1.call-update) | async-done | bytes 46137360 | tf_op jit(solution)/shard_map/all_gather | solution.py:100
  685.4 25.0 %fusion.43 = bf16[2,32,8,352]{3,2,0,1:T(8,128)(2,1)S(1)} fusion(bf16[32,2048,352]{1,2,0:T(8,128)(2,1)} %all-gather.11.cloned.1.call-done, bf16[2,32,8,2048]{3,2,1,0:T(8,128)(2,1)S(1)} %all_to_all.19, f32[2,32,8,352]{3,2,0,1:T(8,128)S(1)} %fusion.28), kind=kOutput, calls=%fused_computation.41 | convolution fusion | flops 739278848 | bytes 49315840 | tf_op jit(solution)/shard_map/resd,edf->resf/dot_general | solution.py:119
  710.5 250.0 %all-gather.13.cloned.1.call-done = bf16[32,352,2048]{2,1,0:T(8,128)(2,1)} async-done(((bf16[32,352,512]{2,1,0:T(8,128)(2,1)}), bf16[32,352,2048]{2,1,0:T(8,128)(2,1)}) %all-gather.13.cloned.1.call-update) | async-done | bytes 46137360 | tf_op jit(solution)/shard_map/all_gather | solution.py:101
  960.5 17.5 %fusion.21 = bf16[2,32,8,2048]{3,2,0,1:T(8,128)(2,1)S(1)} fusion(bf16[2,32,8,352]{3,2,0,1:T(8,128)(2,1)S(1)} %fusion.43, bf16[32,352,2048]{2,1,0:T(8,128)(2,1)} %all-gather.13.cloned.1.call-done), kind=kOutput, calls=%fused_computation.32 | convolution fusion | flops 739246080 | bytes 48594944 | tf_op jit(solution)/shard_map/resf,efd->resd/dot_general | solution.py:121
  978.1 28.1 %all_to_all.20 = bf16[2,32,8,2048]{3,2,1,0:T(8,128)(2,1)S(1)} all-to-all(bf16[2,32,8,2048]{3,2,1,0:T(8,128)(2,1)S(1)} %copy.78), channel_id=1, replica_groups=mesh['req'=2,'ctx'=4,'tp'=4] {'req'}, dimensions={0} | all-to-all | bytes 4194304 | tf_op jit(solution)/shard_map/all_to_all | solution.py:124
  1006.2 9.1 copy.79
  1015.3 10.5 reshape.199
  1025.8 4.9 all-to-all-start.2
  1030.9 47.7 %all-to-all-done.2 = bf16[4,2,131072]{2,1,0:T(2,128)(2,1)S(1)} async-done(((bf16[4,2,131072]{2,1,0:T(2,128)(2,1)}), bf16[4,2,131072]{2,1,0:T(2,128)(2,1)S(1)}, u32[]{:S(2)}, u32[]{:S(2)}) %all-to-all-start.2) | async-done | bytes 2097184 | tf_op jit(solution)/shard_map/all_to_all | solution.py:123
  1078.5 5.6 reshape.200
  1084.1 7.5 convert_reduce_fusion
  1091.6 3.2 copy.81
  1094.9 1.6 gather_fusion
  1096.6 0.4 multiply_reduce_fusion
  1097.0 1.6 add_convert_fusion
  (73 shorter events, 3.9 us)
Async XLA Ops:
  6.5 11.3 %copy-start = (bf16[256,4,128]{2,1,0:T(4,128)(2,1)S(1)}, bf16[256,4,128]{2,1,0:T(4,128)(2,1)}, u32[]{:S(2)}) copy-start(bf16[256,4,128]{2,1,0:T(4,128)(2,1)} %param.16) | copy-start | bytes 786436
  6.5 63.2 %all-gather.15.cloned.1.call-start = ((), (), s32[]{:S(2)}) async-start(), calls=%async_computation.8 | async-start | bytes 2621440 | tf_op jit(solution)/shard_map/all_gather | solution.py:13
  12.2 5.6 copy-start.3
  24.7 11.4 %copy-start.8 = (bf16[256,1,128]{2,0,1:T(8,128)(2,1)S(1)}, bf16[256,1,128]{2,0,1:T(8,128)(2,1)}, u32[]{:S(2)}) copy-start(bf16[256,1,128]{2,0,1:T(8,128)(2,1)} %param.18) | copy-start | bytes 196612
  44.2 49.8 %all-gather.7.cloned.1.call-start = ((), (), s32[]{:S(2)}) async-start(), calls=%async_computation.3 | async-start | bytes 2621440 | tf_op jit(solution)/shard_map/all_gather | solution.py:88
  44.9 90.4 %all-reduce.2.cloned.1.call-start = ((), (), s32[]{:S(2)}) async-start(), calls=%async_computation.4 | async-start | bytes 1048576 | tf_op jit(solution)/shard_map/psum | solution.py:95
  70.8 1.4 slice-start
  77.1 18.8 %copy-start.4 = (bf16[64,512]{1,0:T(8,128)(2,1)S(1)}, bf16[64,512]{1,0:T(8,128)(2,1)}, u32[]{:S(2)}) copy-start(bf16[64,512]{1,0:T(8,128)(2,1)} %param.22) | copy-start | bytes 196612
  96.0 0.8 copy-start.2
  96.8 313.5 %all-gather.9.cloned.1.call-start = ((), (), s32[]{:S(2)}) async-start(), calls=%async_computation.5 | async-start | bytes 57671680 | tf_op jit(solution)/shard_map/all_gather | solution.py:99
  97.4 588.0 %all-gather.11.cloned.1.call-start = ((), (), s32[]{:S(2)}) async-start(), calls=%async_computation.6 | async-start | bytes 57671680 | tf_op jit(solution)/shard_map/all_gather | solution.py:100
  98.0 0.7 copy-start.5
  98.0 38.5 %copy-start.6 = (f32[2048]{0:T(1024)S(1)}, f32[2048]{0:T(1024)}, u32[]{:S(2)}) copy-start(f32[2048]{0:T(1024)} %param.24) | copy-start | bytes 24580
  98.0 862.5 %all-gather.13.cloned.1.call-start = ((), (), s32[]{:S(2)}) async-start(), calls=%async_computation.7 | async-start | bytes 57671680 | tf_op jit(solution)/shard_map/all_gather | solution.py:101
  1025.8 5.0 copy-start.7
  1025.8 52.7 %all-to-all-start.2 = ((bf16[4,2,131072]{2,1,0:T(2,128)(2,1)}), bf16[4,2,131072]{2,1,0:T(2,128)(2,1)S(1)}, u32[]{:S(2)}, u32[]{:S(2)}) async-start(bf16[4,2,131072]{2,1,0:T(2,128)(2,1)} %reshape.199), calls=%async_computation.2 | async-start | bytes 4194304 | tf_op jit(solution)/shard_map/all_to_all | solution.py:123
  1094.9 3.7 copy-start.1
Sparse Core Ops, SparseCore 0:
  44.3 25.3 all-gather.14
  71.3 22.6 all-gather.6
  97.0 38.2 all-reduce.1
  136.7 273.5 all-gather.8
  411.8 273.5 all-gather.10
  686.9 273.5 all-gather.12
where the time goes:
time: 1110 us
  waiting for transfers between devices  843 us (76%)
  matrix products  84 us (8%)
  blocking collectives  68.4 us (6%)
  local copies, waits for them, and re-layouts  67.8 us (6%)
  other arithmetic  23.1 us (2%)
  between operations  14 us (1%)
    all_gather x1, waiting for transfers between devices, body(): lax.all_gather(w_up, 'ctx', axis=1, tiled=True)  250 us
    all_gather x1, waiting for transfers between devices, body(): lax.all_gather(w_down, 'ctx', axis=2, tiled=True)  250 us
    all_gather x1, waiting for transfers between devices, body(): lax.all_gather(w_gate, 'ctx', axis=1, tiled=True)  235 us
    all_to_all x1, waiting for transfers between devices, body(): lax.all_to_all(lax.all_to_all(expert_out, 'req', split_axis=0, concat_axi...  47.7 us
    psum x1, waiting for transfers between devices, body(): hidden = lax.psum(partial_value, 'tp')  34.6 us
    all_to_all x1, blocking collectives, body(): lax.all_to_all(outgoing, 'req', split_axis=0, concat_axis=0, tiled=True)  28.3 us
    all_to_all x1, blocking collectives, body(): lax.all_to_all(expert_out, 'req', split_axis=0, concat_axis=0, tiled=True)  28.1 us
    dot_general x1, matrix products, body(): jnp.einsum('resd,edf->resf', gathered, full_up, preferred_element_type=jn...  25 us
  transfers between devices with their start and end apart: 7, of which 7 were waited for; matrix products, arithmetic and copies ran while one was open for 7% of the time, Pallas kernels for 0%

commit v1 on v0

--- a/solution.py
+++ b/solution.py
@@ -120,12 +120,20 @@
     inner = (jax.nn.silu(gate_act) * up_act).astype(jnp.bfloat16)
     down_act = jnp.einsum("resf,efd->resd", inner, full_down, preferred_element_type=jnp.float32)
     expert_out = down_act.astype(jnp.bfloat16)
-    returned_rows = lax.all_to_all(
-        lax.all_to_all(expert_out, "req", split_axis=0, concat_axis=0, tiled=True),
-        "tp",
-        split_axis=3,
-        concat_axis=2,
-        tiled=True,
+    returned_rows = jnp.concatenate(
+        lax.all_to_all(
+            jnp.stack(
+                jnp.split(
+                    lax.all_to_all(expert_out, "req", split_axis=0, concat_axis=0, tiled=True),
+                    lax.axis_size("tp"),
+                    axis=3,
+                )
+            ),
+            "tp",
+            0,
+            0,
+        ),
+        axis=2,
     )
     slot_sums = (
         returned_rows.reshape(req_count, exp_dev, tp_count, CAP, d_share).astype(jnp.float32).sum(2)

time: 1110 us -> 1070 us (0.964)
  local copies, waits for them, and re-layouts: 67.8 us -> 39.5 us
    unnamed x22 -> x20, local copies, waits for them, and re-layouts: 17.2 us -> 1.1 us
where the time goes in v1:
time: 1070 us
  waiting for transfers between devices  843 us (79%)
  matrix products  84 us (8%)
  blocking collectives  68.2 us (6%)
  local copies, waits for them, and re-layouts  39.5 us (4%)
  other arithmetic  17.5 us (2%)
  between operations  13.8 us (1%)
    all_gather x1, waiting for transfers between devices, body(): lax.all_gather(w_up, 'ctx', axis=1, tiled=True)  250 us
    all_gather x1, waiting for transfers between devices, body(): lax.all_gather(w_down, 'ctx', axis=2, tiled=True)  250 us
    all_gather x1, waiting for transfers between devices, body(): lax.all_gather(w_gate, 'ctx', axis=1, tiled=True)  235 us
    all_to_all x1, waiting for transfers between devices, body(): lax.all_to_all(jnp.stack(jnp.split(lax.all_to_all(expert_out, 'req', spli...  47.7 us
    psum x1, waiting for transfers between devices, body(): hidden = lax.psum(partial_value, 'tp')  34.6 us
    all_to_all x1, blocking collectives, body(): lax.all_to_all(outgoing, 'req', split_axis=0, concat_axis=0, tiled=True)  28.3 us
    all_to_all x1, blocking collectives, body(): lax.all_to_all(expert_out, 'req', split_axis=0, concat_axis=0, tiled=True)  28.1 us
    dot_general x1, matrix products, body(): jnp.einsum('resd,edf->resf', gathered, full_up, preferred_element_type=jn...  25 us
  transfers between devices with their start and end apart: 7, of which 7 were waited for; matrix products, arithmetic and copies ran while one was open for 7% of the time, Pallas kernels for 0%

profile of v1, /device:TPU:0, one launch (start us, length us, event | category | flops | bytes accessed | tf_op | source)
XLA Modules:
  0.0 1071.4 jit_solution(12354337486215563970)
XLA Ops:
  6.6 1.3 dynamic_slice.24
  7.9 0.7 add_compare_fusion
  8.5 0.2 pad_add_fusion
  8.7 3.5 broadcast_in_dim.48.clone
  12.2 5.6 broadcast_in_dim.49
  17.8 6.7 fusion.14
  24.7 11.4 %reshape.148 = f32[256,4,2304]{2,1,0:T(4,128)} reshape(f32[1024,2304]{1,0:T(8,128)} %get-tuple-element.89) | data formatting | bytes 18874368 | tf_op jit(solution)/shard_map/reshape | solution.py:69
  36.1 8.0 fusion.15
  44.2 0.7 all-gather.7.cloned.1.call-update
  45.1 5.3 select_reduce_fusion
  50.6 6.2 all_gather.33
  56.9 5.6 all_gather.31
  62.5 7.2 all-gather.15.cloned.1.call-done
  69.7 1.1 slice.40
  70.8 0.3 copy.48
  71.1 1.1 slice-done
  72.2 4.9 while.14
  72.5 1.3 fusion.75
  74.2 1.3 fusion.75
  75.9 1.3 fusion.75
  77.5 16.4 %all-gather.7.cloned.1.call-done = bf16[512,2048]{1,0:T(8,128)(2,1)} async-done(((bf16[512,512]{1,0:T(8,128)(2,1)}), bf16[512,2048]{1,0:T(8,128)(2,1)}) %all-gather.7.cloned.1.call-update) | async-done | bytes 2097168 | tf_op jit(solution)/shard_map/all_gather | solution.py:88
  93.9 2.1 fusion.59
  96.0 0.8 copy-done.2
  96.9 0.5 all-gather.9.cloned.1.call-update
  97.5 0.5 all-gather.11.cloned.1.call-update
  98.1 0.5 all-gather.13.cloned.1.call-update
  99.1 0.9 reduce-window.6
  100.0 0.2 slice_reduce_fusion
  100.7 34.6 %all-reduce.2.cloned.1.call-done = f32[64,2048]{1,0:T(8,128)} async-done(((f32[64,2048]{1,0:T(8,128)}), f32[64,2048]{1,0:T(8,128)}) %all-reduce.2.cloned.1.call-update) | async-done | bytes 524304 | tf_op jit(solution)/shard_map/psum | solution.py:95
  135.3 1.2 multiply_reduce_fusion.1
  136.5 1.2 multiply_convert_fusion
  137.7 9.7 scatter_custom_fusion
  147.3 28.3 %all_to_all.15 = bf16[2,32,8,2048]{3,2,1,0:T(8,128)(2,1)S(1)} all-to-all(bf16[2,32,8,2048]{3,2,1,0:T(8,128)(2,1)} %bitcast.110), channel_id=1, replica_groups=mesh['req'=2,'ctx'=4,'tp'=4] {'req'}, dimensions={0} | all-to-all | bytes 4194304 | tf_op jit(solution)/shard_map/all_to_all | solution.py:117
  175.6 234.7 %all-gather.9.cloned.1.call-done = bf16[32,2048,352]{1,2,0:T(8,128)(2,1)} async-done(((bf16[32,512,352]{1,2,0:T(8,128)(2,1)}), bf16[32,2048,352]{1,2,0:T(8,128)(2,1)}) %all-gather.9.cloned.1.call-update) | async-done | bytes 46137360 | tf_op jit(solution)/shard_map/all_gather | solution.py:99
  410.4 24.8 %fusion.28 = f32[2,32,8,352]{3,2,0,1:T(8,128)S(1)} fusion(bf16[32,2048,352]{1,2,0:T(8,128)(2,1)} %all-gather.9.cloned.1.call-done, bf16[2,32,8,2048]{3,2,1,0:T(8,128)(2,1)S(1)} %all_to_all.15), kind=kOutput, calls=%fused_computation.39 | convolution fusion | flops 738197504 | bytes 48955392 | tf_op jit(solution)/shard_map/resd,edf->resf/dot_general | solution.py:118
  435.1 250.3 %all-gather.11.cloned.1.call-done = bf16[32,2048,352]{1,2,0:T(8,128)(2,1)} async-done(((bf16[32,512,352]{1,2,0:T(8,128)(2,1)}), bf16[32,2048,352]{1,2,0:T(8,128)(2,1)}) %all-gather.11.cloned.1.call-update) | async-done | bytes 46137360 | tf_op jit(solution)/shard_map/all_gather | solution.py:100
  685.4 25.0 %fusion.43 = bf16[2,32,8,352]{3,2,0,1:T(8,128)(2,1)S(1)} fusion(bf16[32,2048,352]{1,2,0:T(8,128)(2,1)} %all-gather.11.cloned.1.call-done, bf16[2,32,8,2048]{3,2,1,0:T(8,128)(2,1)S(1)} %all_to_all.15, f32[2,32,8,352]{3,2,0,1:T(8,128)S(1)} %fusion.28), kind=kOutput, calls=%fused_computation.42 | convolution fusion | flops 739278848 | bytes 49315840 | tf_op jit(solution)/shard_map/resd,edf->resf/dot_general | solution.py:119
  710.5 250.0 %all-gather.13.cloned.1.call-done = bf16[32,352,2048]{2,1,0:T(8,128)(2,1)} async-done(((bf16[32,352,512]{2,1,0:T(8,128)(2,1)}), bf16[32,352,2048]{2,1,0:T(8,128)(2,1)}) %all-gather.13.cloned.1.call-update) | async-done | bytes 46137360 | tf_op jit(solution)/shard_map/all_gather | solution.py:101
  960.5 17.5 %fusion.21 = bf16[2,32,8,2048]{3,2,0,1:T(8,128)(2,1)S(1)} fusion(bf16[2,32,8,352]{3,2,0,1:T(8,128)(2,1)S(1)} %fusion.43, bf16[32,352,2048]{2,1,0:T(8,128)(2,1)} %all-gather.13.cloned.1.call-done), kind=kOutput, calls=%fused_computation.32 | convolution fusion | flops 739246080 | bytes 48594944 | tf_op jit(solution)/shard_map/resf,efd->resd/dot_general | solution.py:121
  978.1 28.1 %all_to_all.16 = bf16[2,32,8,2048]{3,2,1,0:T(8,128)(2,1)S(1)} all-to-all(bf16[2,32,8,2048]{3,2,1,0:T(8,128)(2,1)S(1)} %copy.57), channel_id=1, replica_groups=mesh['req'=2,'ctx'=4,'tp'=4] {'req'}, dimensions={0} | all-to-all | bytes 4194304 | tf_op jit(solution)/shard_map/all_to_all | solution.py:127
  1006.2 0.2 slice_bitcast_fusion.3
  1006.4 1.6 pad_maximum_fusion
  1008.0 4.7 all-to-all-start.2
  1012.8 47.7 %all-to-all-done.2 = bf16[4,2,32,8,512]{4,3,2,1,0:T(8,128)(2,1)S(1)} async-done(((bf16[4,2,32,8,512]{4,3,2,1,0:T(8,128)(2,1)}), bf16[4,2,32,8,512]{4,3,2,1,0:T(8,128)(2,1)S(1)}, u32[]{:S(2)}, u32[]{:S(2)}) %all-to-all-start.2) | async-done | bytes 2097184 | tf_op jit(solution)/shard_map/all_to_all | solution.py:124
  1060.5 0.3 convert_reduce_fusion
  1060.9 1.6 gather_fusion
  1062.6 0.4 multiply_reduce_fusion
  1063.0 1.6 add_convert_fusion
  (71 shorter events, 3.5 us)
Async XLA Ops:
  6.5 11.3 %copy-start = (bf16[256,4,128]{2,1,0:T(4,128)(2,1)S(1)}, bf16[256,4,128]{2,1,0:T(4,128)(2,1)}, u32[]{:S(2)}) copy-start(bf16[256,4,128]{2,1,0:T(4,128)(2,1)} %param.16) | copy-start | bytes 786436
  6.5 63.2 %all-gather.15.cloned.1.call-start = ((), (), s32[]{:S(2)}) async-start(), calls=%async_computation.8 | async-start | bytes 2621440 | tf_op jit(solution)/shard_map/all_gather | solution.py:13
  12.2 5.6 copy-start.3
  24.7 11.4 %copy-start.8 = (bf16[256,1,128]{2,0,1:T(8,128)(2,1)S(1)}, bf16[256,1,128]{2,0,1:T(8,128)(2,1)}, u32[]{:S(2)}) copy-start(bf16[256,1,128]{2,0,1:T(8,128)(2,1)} %param.18) | copy-start | bytes 196612
  44.2 49.8 %all-gather.7.cloned.1.call-start = ((), (), s32[]{:S(2)}) async-start(), calls=%async_computation.3 | async-start | bytes 2621440 | tf_op jit(solution)/shard_map/all_gather | solution.py:88
  44.9 90.4 %all-reduce.2.cloned.1.call-start = ((), (), s32[]{:S(2)}) async-start(), calls=%async_computation.4 | async-start | bytes 1048576 | tf_op jit(solution)/shard_map/psum | solution.py:95
  70.8 1.4 slice-start
  77.1 18.8 %copy-start.4 = (bf16[64,512]{1,0:T(8,128)(2,1)S(1)}, bf16[64,512]{1,0:T(8,128)(2,1)}, u32[]{:S(2)}) copy-start(bf16[64,512]{1,0:T(8,128)(2,1)} %param.22) | copy-start | bytes 196612
  96.0 0.8 copy-start.2
  96.8 313.5 %all-gather.9.cloned.1.call-start = ((), (), s32[]{:S(2)}) async-start(), calls=%async_computation.5 | async-start | bytes 57671680 | tf_op jit(solution)/shard_map/all_gather | solution.py:99
  97.4 588.0 %all-gather.11.cloned.1.call-start = ((), (), s32[]{:S(2)}) async-start(), calls=%async_computation.6 | async-start | bytes 57671680 | tf_op jit(solution)/shard_map/all_gather | solution.py:100
  98.0 0.7 copy-start.5
  98.0 38.5 %copy-start.6 = (f32[2048]{0:T(1024)S(1)}, f32[2048]{0:T(1024)}, u32[]{:S(2)}) copy-start(f32[2048]{0:T(1024)} %param.24) | copy-start | bytes 24580
  98.0 862.5 %all-gather.13.cloned.1.call-start = ((), (), s32[]{:S(2)}) async-start(), calls=%async_computation.7 | async-start | bytes 57671680 | tf_op jit(solution)/shard_map/all_gather | solution.py:101
  1008.0 4.7 copy-start.7
  1008.0 52.5 %all-to-all-start.2 = ((bf16[4,2,32,8,512]{4,3,2,1,0:T(8,128)(2,1)}), bf16[4,2,32,8,512]{4,3,2,1,0:T(8,128)(2,1)S(1)}, u32[]{:S(2)}, u32[]{:S(2)}) async-start(bf16[4,2,32,8,512]{4,3,2,1,0:T(8,128)(2,1)} %pad_maximum_fusion), calls=%async_computation.2 | async-start | bytes 4194304 | tf_op jit(solution)/shard_map/all_to_all | solution.py:124
  1060.9 3.7 copy-start.1
Sparse Core Ops, SparseCore 0:
  44.3 25.3 all-gather.14
  71.3 22.6 all-gather.6
  97.0 38.2 all-reduce.1
  136.7 273.5 all-gather.8
  411.8 273.5 all-gather.10
  686.9 273.5 all-gather.12
